TPU v7x, 32 devices: a whole 2x2x4 slice. The times are simulated.
32 devices in a mesh: ckpt: 2 (over y), key: 4 (over x, core), qry: 4 (over z).
Axes of the slice: x: 2, y: 2, z: 4, core: 2. Of those that a mesh axis runs over, the one named last changes fastest.
Arguments:
- queries: bfloat16 [1024, 4096], P(('ckpt', 'qry'), 'key'), parts along dimension 0, may hold values from -8 to 8
- keys: bfloat16 [8192, 1024], P(('ckpt', 'key')), parts along dimension 0, may hold values from -8 to 8
- values: bfloat16 [8192, 1024], P(('ckpt', 'key')), parts along dimension 0, may hold values from -6 to 6
- out_grad: bfloat16 [1024, 4096], P(('ckpt', 'qry'), 'key'), parts along dimension 0, may hold values from -6 to 6
Outputs:
- attn_out: bfloat16 [1024, 4096], P(('ckpt', 'qry'), 'key'), parts along dimension 0
- query_out: bfloat16 [1024, 4096], P(('ckpt', 'qry'), 'key'), parts along dimension 0
- key_out: bfloat16 [8192, 1024], P(('ckpt', 'key'), 'qry'), parts along dimension 0
- value_out: bfloat16 [8192, 1024], P(('ckpt', 'key'), 'qry'), parts along dimension 0
There are 2 independent parts, one for each index of `ckpt`. A program takes and returns all parts, laid end to end along the dimension named above; each array names one. Nothing has to cross between parts.
All inputs are finite; a program needn't handle non-finite values.
Results may differ from a plain program's by a relative error of at most 0.03.
Values may be sent and summed in bfloat16 or wider, within the bound.
A program may use at most 64 MiB of HBM per device.

v0:
```python
import math

import jax
import jax.numpy as jnp
from jax import lax
from jax.sharding import PartitionSpec as P

HQ = 32
KVH = 8
HD = 128


def rounded_values(value):
    return lax.optimization_barrier(value.astype(jnp.bfloat16)).astype(jnp.float32)


def logits_of(query_part, key_part, factor):
    return (
        jnp.einsum("grd,kd->grk", query_part, key_part, preferred_element_type=jnp.float32) * factor
    )


def backward_core(query_part, grad_part, log_norm, row_delta, key_part, value_portion, factor):
    probs = jnp.exp(logits_of(query_part, key_part, factor) - log_norm[..., None])
    grad_prob = jnp.einsum(
        "grd,kd->grk", grad_part, value_portion, preferred_element_type=jnp.float32
    )
    grad_logit = (probs * (grad_prob - row_delta[..., None])).astype(jnp.bfloat16)
    return (probs, grad_logit)


def kv_from(probs, grad_logit, query_part, grad_part, factor):
    value_grad = jnp.einsum(
        "grk,grd->kd", probs.astype(jnp.bfloat16), grad_part, preferred_element_type=jnp.float32
    )
    key_grad = (
        jnp.einsum("grk,grd->kd", grad_logit, query_part, preferred_element_type=jnp.float32)
        * factor
    )
    return (key_grad, value_grad)


def kv_grads(query_part, grad_part, log_norm, row_delta, key_part, value_portion, factor):
    probs, grad_logit = backward_core(
        query_part, grad_part, log_norm, row_delta, key_part, value_portion, factor
    )
    return kv_from(probs, grad_logit, query_part, grad_part, factor)


def per_device(queries, keys, values, out_grad):
    factor = 1.0 / math.sqrt(HD)
    per_group = HQ // KVH
    query_rows, grad_rows = (
        lax.all_gather(queries, "key", axis=1, tiled=True),
        lax.all_gather(out_grad, "key", axis=1, tiled=True),
    )
    row_count = query_rows.shape[0]
    key_count = keys.shape[0]
    query_heads = query_rows.reshape(row_count, KVH, per_group, HD).transpose(1, 2, 0, 3)
    grad_heads = grad_rows.reshape(row_count, KVH, per_group, HD).transpose(1, 2, 0, 3)
    key_heads = keys.reshape(key_count, KVH, HD).transpose(1, 0, 2)
    value_heads = values.reshape(key_count, KVH, HD).transpose(1, 0, 2)

    def block_forward_pass(inputs):
        query_part, key_part, value_portion = inputs
        logits = logits_of(query_part, key_part, factor)
        local_peak = jnp.max(logits, axis=-1)
        exponent_terms = jnp.exp(logits - local_peak[..., None])
        summed = jnp.einsum(
            "grk,kd->grd",
            exponent_terms.astype(jnp.bfloat16),
            value_portion,
            preferred_element_type=jnp.float32,
        )
        return (local_peak, jnp.sum(exponent_terms, axis=-1), summed)

    local_peak, local_sum, summed = lax.map(
        block_forward_pass, (query_heads, key_heads, value_heads)
    )
    peak = lax.pmax(local_peak, "key")
    weight = jnp.exp(local_peak - peak)
    totals = lax.psum(local_sum * weight, "key")
    log_norm = peak + jnp.log(totals)
    scaled = summed * (weight / totals)[..., None]
    partial_value = scaled.transpose(2, 0, 1, 3).reshape(row_count, HQ * HD)
    attn_out = lax.psum_scatter(
        partial_value.astype(jnp.bfloat16), "key", scatter_dimension=1, tiled=True
    )
    products = out_grad.astype(jnp.float32) * attn_out.astype(jnp.float32)
    own_delta = jnp.sum(products.reshape(row_count, -1, HD), axis=-1)
    row_delta = lax.all_gather(own_delta, "key", axis=1, tiled=True)
    delta_heads = row_delta.T.reshape(KVH, per_group, row_count)
    backward_inputs = (query_heads, grad_heads, log_norm, delta_heads, key_heads, value_heads)

    def query_only(inputs):
        probs, grad_logit = backward_core(*inputs, factor)
        return (
            jnp.einsum("grk,kd->grd", grad_logit, inputs[4], preferred_element_type=jnp.float32)
            * factor
        )

    query_grad = lax.map(query_only, backward_inputs)
    n_qry = lax.axis_size("qry")
    kv_local = KVH // n_qry
    query_mine, grad_mine = (
        lax.all_to_all(query_rows, "qry", split_axis=1, concat_axis=0, tiled=True),
        lax.all_to_all(grad_rows, "qry", split_axis=1, concat_axis=0, tiled=True),
    )
    norm_mine, delta_mine = (
        lax.all_to_all(
            log_norm.reshape(HQ, row_count), "qry", split_axis=0, concat_axis=1, tiled=True
        ),
        lax.all_to_all(
            delta_heads.reshape(HQ, row_count), "qry", split_axis=0, concat_axis=1, tiled=True
        ),
    )
    start = lax.axis_index("qry") * kv_local
    key_mine = lax.dynamic_slice_in_dim(key_heads, start, kv_local, 0)
    value_mine = lax.dynamic_slice_in_dim(value_heads, start, kv_local, 0)

    def split_rows(stacked):
        return stacked.reshape(n_qry, row_count, kv_local, per_group, HD).transpose(0, 2, 3, 1, 4)

    def split_stats(stacked):
        return stacked.reshape(kv_local, per_group, n_qry, row_count).transpose(2, 0, 1, 3)

    def per_block(running, pieces):
        key_grad, value_grad = jax.vmap(kv_grads, in_axes=(0, 0, 0, 0, 0, 0, None))(
            pieces[0], pieces[1], pieces[2], pieces[3], key_mine, value_mine, factor
        )
        return (
            (running[0] + rounded_values(key_grad), running[1] + rounded_values(value_grad)),
            None,
        )

    empty = jnp.zeros((kv_local, key_count, HD), jnp.float32)
    sums, unused = lax.scan(
        per_block,
        (empty, empty),
        (
            split_rows(query_mine),
            split_rows(grad_mine),
            split_stats(norm_mine),
            split_stats(delta_mine),
        ),
    )
    key_out = sums[0].transpose(1, 0, 2).reshape(key_count, kv_local * HD)
    value_out = sums[1].transpose(1, 0, 2).reshape(key_count, kv_local * HD)
    query_flat = query_grad.transpose(2, 0, 1, 3).reshape(row_count, HQ * HD)
    query_out = lax.psum_scatter(
        query_flat.astype(jnp.bfloat16), "key", scatter_dimension=1, tiled=True
    )
    return (attn_out, query_out, key_out.astype(jnp.bfloat16), value_out.astype(jnp.bfloat16))


def solution(mesh):
    in_specs = (
        P(("ckpt", "qry"), "key"),
        P(("ckpt", "key"), None),
        P(("ckpt", "key"), None),
        P(("ckpt", "qry"), "key"),
    )
    out_specs = (
        P(("ckpt", "qry"), "key"),
        P(("ckpt", "qry"), "key"),
        P(("ckpt", "key"), "qry"),
        P(("ckpt", "key"), "qry"),
    )
    return jax.shard_map(
        per_device, mesh=mesh, in_specs=in_specs, out_specs=out_specs, check_vma=False
    )
```

profile of v0, /device:TPU:29, one launch (start us, length us, event | category | flops | bytes accessed | tf_op | source)
XLA Modules:
  0.0 256.6 jit_solution(14281453036364921101)
XLA Ops:
  10.9 2.9 %copy.84 = bf16[1024,1024]{0,1:T(8,128)(2,1)S(1)} copy(bf16[1024,1024]{1,0:T(8,128)(2,1)} %param.11) | data formatting | bytes 4194304 | tf_op args[1]
  13.8 2.4 copy.87
  16.2 3.9 %copy.85 = bf16[1024,1024]{0,1:T(8,128)(2,1)} copy(bf16[1024,1024]{1,0:T(8,128)(2,1)} %param.12) | data formatting | bytes 4194304 | tf_op args[2]
  20.1 3.9 %copy.88 = bf16[8,1024,128]{2,1,0:T(8,128)(2,1)} copy(bf16[8,1024,128]{1,2,0:T(8,128)(2,1)} %bitcast.233) | data formatting | bytes 4194304 | tf_op jit(solution)/shard_map/while | solution.py:77
  24.0 4.1 %all-gather.3.cloned.1.call-done = bf16[128,4096]{0,1:T(8,128)(2,1)} async-done(((bf16[128,1024]{0,1:T(8,128)(2,1)}), bf16[128,4096]{0,1:T(8,128)(2,1)}) %all-gather.3.cloned.1.call-update) | async-done | bytes 1048592 | tf_op jit(solution)/shard_map/all_gather | solution.py:54
  29.8 33.5 %while.40 = (s32[]{:T(128)}, f32[8,4,128]{2,1,0:T(4,128)S(1)}, f32[8,4,128]{2,1,0:T(4,128)S(1)}, f32[8,4,128,128]{3,2,1,0:T(8,128)}, bf16[8,4,128,128]{3,2,1,0:T...) while((s32[]{:T(128)}, f32[8,4,128]{2,1,0:T(4,128)S(1)}, ...), condition=%wide.region_3.4_spmd.clone, body=%wide.region_0.3_spmd.sunk.clone | while | flops 272628736 | bytes 7227481 | solution.py:77
  63.3 9.4 %pmax.7 = f32[8,4,128]{2,1,0:T(4,128)S(1)} all-reduce(f32[8,4,128]{2,1,0:T(4,128)S(1)} %get-tuple-element.134), channel_id=1, replica_groups=mesh['ckpt'=2,'key'=4,'qry'=4] {'key'}, use_global_device_ids=true, to_apply=%region_4.5 | all-reduce | flops 4096 | bytes 32768 | tf_op jit(solution)/shard_map/pmax | solution.py:80
  72.7 10.2 %psum.7 = f32[8,4,128]{2,1,0:T(4,128)S(1)} all-reduce(f32[8,4,128]{2,1,0:T(4,128)S(1)} %bitcast.251), channel_id=1, replica_groups=mesh['ckpt'=2,'key'=4,'qry'=4] {'key'}, use_global_device_ids=true, to_apply=%region_5.6 | all-reduce | flops 4096 | bytes 32768 | tf_op jit(solution)/shard_map/psum | solution.py:82
  83.0 5.9 %all_to_all.64 = f32[4,8,128]{2,1,0:T(8,128)S(1)} all-to-all(f32[4,8,128]{2,1,0:T(8,128)S(1)} %get-tuple-element.349), channel_id=1, replica_groups=mesh['ckpt'=2,'key'=4,'qry'=4] {'qry'}, dimensions={0} | all-to-all | bytes 32768 | tf_op jit(solution)/shard_map/all_to_all | solution.py:110
  88.9 6.4 %all-to-all-start = ((bf16[128,4,1024]{0,2,1:T(8,128)(2,1)}), bf16[128,4,1024]{0,2,1:T(8,128)(2,1)S(1)}, u32[]{:S(2)}, u32[]{:S(2)}) async-start(bf16[128,4,1024]{0,2,1:T(8,128)(2,1)} %bitcast.237), calls=%async_computation.2 | async-start | bytes 2097152 | tf_op jit(solution)/shard_map/all_to_all | solution.py:106
  99.0 2.6 %convert_element_type.68 = bf16[128,4096]{1,0:T(8,128)(2,1)} reshape(bf16[128,8,4,128]{3,2,1,0:T(4,128)(2,1)} %copy.89) | data formatting | bytes 2097152 | tf_op jit(solution)/shard_map/convert_element_type | solution.py:87
  101.7 14.7 %all-to-all-done = bf16[128,4,1024]{0,2,1:T(8,128)(2,1)S(1)} async-done(((bf16[128,4,1024]{0,2,1:T(8,128)(2,1)}), bf16[128,4,1024]{0,2,1:T(8,128)(2,1)S(1)}, u32[]{:S(2)}, u32[]{:S(2)}) %all-to-all-start) | async-done | bytes 1048608 | tf_op jit(solution)/shard_map/all_to_all | solution.py:106
  116.4 8.4 %all-to-all-start.2 = ((bf16[128,4,1024]{0,2,1:T(8,128)(2,1)}), bf16[128,4,1024]{0,2,1:T(8,128)(2,1)}, u32[]{:S(2)}, u32[]{:S(2)}) async-start(bf16[128,4,1024]{0,2,1:T(8,128)(2,1)} %bitcast.240), calls=%async_computation.4 | async-start | bytes 2097152 | tf_op jit(solution)/shard_map/all_to_all | solution.py:107
  133.6 7.1 %all_gather.11 = f32[128,32]{0,1:T(8,128)} all-gather(f32[128,8]{0,1:T(8,128)S(1)} %copy.91), channel_id=1, replica_groups=mesh['ckpt'=2,'key'=4,'qry'=4] {'key'}, dimensions={1}, use_global_device_ids=true | all-gather | bytes 20480 | tf_op jit(solution)/shard_map/all_gather | solution.py:91
  140.8 6.5 %all-to-all-done.2 = bf16[128,4,1024]{0,2,1:T(8,128)(2,1)} async-done(((bf16[128,4,1024]{0,2,1:T(8,128)(2,1)}), bf16[128,4,1024]{0,2,1:T(8,128)(2,1)}, u32[]{:S(2)}, u32[]{:S(2)}) %all-to-all-start.2) | async-done | bytes 1048608 | tf_op jit(solution)/shard_map/all_to_all | solution.py:107
  147.2 6.2 %all-to-all-start.3 = ((f32[4,8,128]{2,1,0:T(8,128)}), f32[4,8,128]{2,1,0:T(8,128)S(1)}, u32[]{:S(2)}, u32[]{:S(2)}) async-start(f32[4,8,128]{2,1,0:T(8,128)} %bitcast.46), calls=%async_computation.5 | async-start | bytes 32768 | tf_op jit(solution)/shard_map/all_to_all | solution.py:113
  153.4 37.7 %while.41 = (s32[]{:T(128)}, bf16[8,4,128,128]{3,2,1,0:T(8,128)(2,1)}, bf16[8,4,128,128]{3,2,1,0:T(8,128)(2,1)}, bf16[8,1024,128]{2,1,0:T(8,128)(2,1)}, f32[8,4,...) while((s32[]{:T(128)}, ...), condition=%wide.region_9.10_spmd.clone, body=%wide.region_8.9_spmd.sunk.clone | while | flops 405340160 | bytes 5520481 | solution.py:102
  155.5 2.6 %fusion.132 = bf16[8,4,128,128]{3,2,1,0:T(8,128)(2,1)} fusion(bf16[8,4,128,128]{3,2,1,0:T(8,128)(2,1)} %get-tuple-element.583, s32[]{:T(128)S(6)} %copy.135, f32[4,128,1024]{2,1,0:T(8,128)S(1)} %fusion.131, f32[4,128]{1,0:T(4,128)S(1)} %get-tuple-element.519, f32[4,128]{1,0:T(4,128)S(1)} %get-tuple-element.520, ...), kind=kOutput, calls=%fused_computation.24.clone.1.clone | convolution fusion | flops 271122432 | bytes 3020800 | tf_op jit(solution)/shard_map/while/body/eval_jaxpr/grk,kd->grd/dot_general | solution.py:98
  160.3 2.6 %fusion.132 = bf16[8,4,128,128]{3,2,1,0:T(8,128)(2,1)} fusion(bf16[8,4,128,128]{3,2,1,0:T(8,128)(2,1)} %get-tuple-element.583, s32[]{:T(128)S(6)} %copy.135, f32[4,128,1024]{2,1,0:T(8,128)S(1)} %fusion.131, f32[4,128]{1,0:T(4,128)S(1)} %get-tuple-element.519, f32[4,128]{1,0:T(4,128)S(1)} %get-tuple-element.520, ...), kind=kOutput, calls=%fused_computation.24.clone.1.clone | convolution fusion | flops 271122432 | bytes 3020800 | tf_op jit(solution)/shard_map/while/body/eval_jaxpr/grk,kd->grd/dot_general | solution.py:98
  165.0 2.6 %fusion.132 = bf16[8,4,128,128]{3,2,1,0:T(8,128)(2,1)} fusion(bf16[8,4,128,128]{3,2,1,0:T(8,128)(2,1)} %get-tuple-element.583, s32[]{:T(128)S(6)} %copy.135, f32[4,128,1024]{2,1,0:T(8,128)S(1)} %fusion.131, f32[4,128]{1,0:T(4,128)S(1)} %get-tuple-element.519, f32[4,128]{1,0:T(4,128)S(1)} %get-tuple-element.520, ...), kind=kOutput, calls=%fused_computation.24.clone.1.clone | convolution fusion | flops 271122432 | bytes 3020800 | tf_op jit(solution)/shard_map/while/body/eval_jaxpr/grk,kd->grd/dot_general | solution.py:98
  169.7 2.6 %fusion.132 = bf16[8,4,128,128]{3,2,1,0:T(8,128)(2,1)} fusion(bf16[8,4,128,128]{3,2,1,0:T(8,128)(2,1)} %get-tuple-element.583, s32[]{:T(128)S(6)} %copy.135, f32[4,128,1024]{2,1,0:T(8,128)S(1)} %fusion.131, f32[4,128]{1,0:T(4,128)S(1)} %get-tuple-element.519, f32[4,128]{1,0:T(4,128)S(1)} %get-tuple-element.520, ...), kind=kOutput, calls=%fused_computation.24.clone.1.clone | convolution fusion | flops 271122432 | bytes 3020800 | tf_op jit(solution)/shard_map/while/body/eval_jaxpr/grk,kd->grd/dot_general | solution.py:98
  174.4 2.6 %fusion.132 = bf16[8,4,128,128]{3,2,1,0:T(8,128)(2,1)} fusion(bf16[8,4,128,128]{3,2,1,0:T(8,128)(2,1)} %get-tuple-element.583, s32[]{:T(128)S(6)} %copy.135, f32[4,128,1024]{2,1,0:T(8,128)S(1)} %fusion.131, f32[4,128]{1,0:T(4,128)S(1)} %get-tuple-element.519, f32[4,128]{1,0:T(4,128)S(1)} %get-tuple-element.520, ...), kind=kOutput, calls=%fused_computation.24.clone.1.clone | convolution fusion | flops 271122432 | bytes 3020800 | tf_op jit(solution)/shard_map/while/body/eval_jaxpr/grk,kd->grd/dot_general | solution.py:98
  179.1 2.6 %fusion.132 = bf16[8,4,128,128]{3,2,1,0:T(8,128)(2,1)} fusion(bf16[8,4,128,128]{3,2,1,0:T(8,128)(2,1)} %get-tuple-element.583, s32[]{:T(128)S(6)} %copy.135, f32[4,128,1024]{2,1,0:T(8,128)S(1)} %fusion.131, f32[4,128]{1,0:T(4,128)S(1)} %get-tuple-element.519, f32[4,128]{1,0:T(4,128)S(1)} %get-tuple-element.520, ...), kind=kOutput, calls=%fused_computation.24.clone.1.clone | convolution fusion | flops 271122432 | bytes 3020800 | tf_op jit(solution)/shard_map/while/body/eval_jaxpr/grk,kd->grd/dot_general | solution.py:98
  183.8 2.6 %fusion.132 = bf16[8,4,128,128]{3,2,1,0:T(8,128)(2,1)} fusion(bf16[8,4,128,128]{3,2,1,0:T(8,128)(2,1)} %get-tuple-element.583, s32[]{:T(128)S(6)} %copy.135, f32[4,128,1024]{2,1,0:T(8,128)S(1)} %fusion.131, f32[4,128]{1,0:T(4,128)S(1)} %get-tuple-element.519, f32[4,128]{1,0:T(4,128)S(1)} %get-tuple-element.520, ...), kind=kOutput, calls=%fused_computation.24.clone.1.clone | convolution fusion | flops 271122432 | bytes 3020800 | tf_op jit(solution)/shard_map/while/body/eval_jaxpr/grk,kd->grd/dot_general | solution.py:98
  188.5 2.6 %fusion.132 = bf16[8,4,128,128]{3,2,1,0:T(8,128)(2,1)} fusion(bf16[8,4,128,128]{3,2,1,0:T(8,128)(2,1)} %get-tuple-element.583, s32[]{:T(128)S(6)} %copy.135, f32[4,128,1024]{2,1,0:T(8,128)S(1)} %fusion.131, f32[4,128]{1,0:T(4,128)S(1)} %get-tuple-element.519, f32[4,128]{1,0:T(4,128)S(1)} %get-tuple-element.520, ...), kind=kOutput, calls=%fused_computation.24.clone.1.clone | convolution fusion | flops 271122432 | bytes 3020800 | tf_op jit(solution)/shard_map/while/body/eval_jaxpr/grk,kd->grd/dot_general | solution.py:98
  191.1 3.0 %copy.96 = bf16[128,8,4,128]{3,2,1,0:T(4,128)(2,1)} copy(bf16[128,8,4,128]{3,0,2,1:T(8,128)(2,1)} %bitcast.238) | data formatting | bytes 2097152 | tf_op jit(solution)/shard_map/convert_element_type | solution.py:151
  194.2 2.7 %convert_element_type.73 = bf16[128,4096]{1,0:T(8,128)(2,1)} reshape(bf16[128,8,4,128]{3,2,1,0:T(4,128)(2,1)} %copy.96) | data formatting | bytes 2097152 | tf_op jit(solution)/shard_map/convert_element_type | solution.py:151
  196.9 51.4 %while.42 = (s32[]{:T(128)}, f32[2,1024,128]{2,1,0:T(8,128)S(1)}, f32[2,1024,128]{2,1,0:T(8,128)S(1)}, bf16[4,2,4,128,128]{3,4,2,1,0:T(8,128)(2,1)}, bf16[2,1024...) while((s32[]{:T(128)}, f32[2,1024,128]{2,1,0:T(8,128)S(1)}, ...), condition=%wide.region_12.13_spmd.clone.clone, body=%wide.region_11.12_spmd.clone.sunk.clone | while | flops 1084489728 | bytes 37778584 | solution.py:137
  203.0 5.4 %fusion.142 = bf16[2,1024,128]{2,1,0:T(8,128)(2,1)} fusion(f32[2,4,128,1024]{3,2,1,0:T(8,128)} %copy-done, f32[2,4,128]{2,1,0:T(4,128)S(1)} %dynamic-slice_bitcast_fusion.14, f32[2,4,128]{2,1,0:T(4,128)S(1)} %dynamic-slice_bitcast_fusion.13, bf16[2,1024,128]{2,1,0:T(8,128)(2,1)} %get-tuple-element.623, ...), kind=kOutput, calls=%fused_computation.54.clone.1.clone | convolution fusion | flops 542638080 | bytes 5776384 | tf_op jit(solution)/shard_map/while/body/eval_jaxpr/vmap(grk,grd->kd)/dot_general | solution.py:37
  216.0 5.2 %fusion.142 = bf16[2,1024,128]{2,1,0:T(8,128)(2,1)} fusion(f32[2,4,128,1024]{3,2,1,0:T(8,128)} %copy-done, f32[2,4,128]{2,1,0:T(4,128)S(1)} %dynamic-slice_bitcast_fusion.14, f32[2,4,128]{2,1,0:T(4,128)S(1)} %dynamic-slice_bitcast_fusion.13, bf16[2,1024,128]{2,1,0:T(8,128)(2,1)} %get-tuple-element.623, ...), kind=kOutput, calls=%fused_computation.54.clone.1.clone | convolution fusion | flops 542638080 | bytes 5776384 | tf_op jit(solution)/shard_map/while/body/eval_jaxpr/vmap(grk,grd->kd)/dot_general | solution.py:37
  228.8 5.2 %fusion.142 = bf16[2,1024,128]{2,1,0:T(8,128)(2,1)} fusion(f32[2,4,128,1024]{3,2,1,0:T(8,128)} %copy-done, f32[2,4,128]{2,1,0:T(4,128)S(1)} %dynamic-slice_bitcast_fusion.14, f32[2,4,128]{2,1,0:T(4,128)S(1)} %dynamic-slice_bitcast_fusion.13, bf16[2,1024,128]{2,1,0:T(8,128)(2,1)} %get-tuple-element.623, ...), kind=kOutput, calls=%fused_computation.54.clone.1.clone | convolution fusion | flops 542638080 | bytes 5776384 | tf_op jit(solution)/shard_map/while/body/eval_jaxpr/vmap(grk,grd->kd)/dot_general | solution.py:37
  241.6 5.2 %fusion.142 = bf16[2,1024,128]{2,1,0:T(8,128)(2,1)} fusion(f32[2,4,128,1024]{3,2,1,0:T(8,128)} %copy-done, f32[2,4,128]{2,1,0:T(4,128)S(1)} %dynamic-slice_bitcast_fusion.14, f32[2,4,128]{2,1,0:T(4,128)S(1)} %dynamic-slice_bitcast_fusion.13, bf16[2,1024,128]{2,1,0:T(8,128)(2,1)} %get-tuple-element.623, ...), kind=kOutput, calls=%fused_computation.54.clone.1.clone | convolution fusion | flops 542638080 | bytes 5776384 | tf_op jit(solution)/shard_map/while/body/eval_jaxpr/vmap(grk,grd->kd)/dot_general | solution.py:37
  (120 shorter events, 100.3 us)
Async XLA Ops:
  7.2 21.0 %all-gather.3.cloned.1.call-start = ((), (), s32[]{:S(2)}) async-start(), calls=%async_computation.6 | async-start | bytes 1310720 | tf_op jit(solution)/shard_map/all_gather | solution.py:54
  9.0 92.7 %all-gather.5.cloned.1.call-start = ((), (), s32[]{:S(2)}) async-start(), calls=%async_computation.8 | async-start | bytes 1310720 | tf_op jit(solution)/shard_map/all_gather | solution.py:55
  63.3 25.6 %copy-start.4 = (bf16[8,4,128,128]{3,2,1,0:T(8,128)(2,1)}, bf16[8,4,128,128]{3,2,1,0:T(8,128)(2,1)S(1)}, u32[]{:S(2)}) copy-start(bf16[8,4,128,128]{3,2,1,0:T(8,128)(2,1)S(1)} %get-tuple-element.632) | copy-start | bytes 3145732
  88.9 27.5 %all-to-all-start = ((bf16[128,4,1024]{0,2,1:T(8,128)(2,1)}), bf16[128,4,1024]{0,2,1:T(8,128)(2,1)S(1)}, u32[]{:S(2)}, u32[]{:S(2)}) async-start(bf16[128,4,1024]{0,2,1:T(8,128)(2,1)} %bitcast.237), calls=%async_computation.2 | async-start | bytes 2097152 | tf_op jit(solution)/shard_map/all_to_all | solution.py:106
  95.3 36.9 %reduce-scatter.3.cloned.1.call-start = ((), (), s32[]{:S(2)}) async-start(), calls=%async_computation.7 | async-start | bytes 1310720 | tf_op jit(solution)/shard_map/reduce_scatter | solution.py:86
  116.4 8.4 %copy-start.3 = (bf16[128,4,1024]{0,2,1:T(8,128)(2,1)}, bf16[128,4,1024]{0,2,1:T(8,128)(2,1)S(1)}, u32[]{:S(2)}) copy-start(bf16[128,4,1024]{0,2,1:T(8,128)(2,1)S(1)} %all-to-all-done) | copy-start | bytes 3145732
  116.4 30.9 %all-to-all-start.2 = ((bf16[128,4,1024]{0,2,1:T(8,128)(2,1)}), bf16[128,4,1024]{0,2,1:T(8,128)(2,1)}, u32[]{:S(2)}, u32[]{:S(2)}) async-start(bf16[128,4,1024]{0,2,1:T(8,128)(2,1)} %bitcast.240), calls=%async_computation.4 | async-start | bytes 2097152 | tf_op jit(solution)/shard_map/all_to_all | solution.py:107
  126.9 5.3 %copy-start.5 = (bf16[128,1024]{1,0:T(8,128)(2,1)S(1)}, bf16[128,1024]{1,0:T(8,128)(2,1)}, u32[]{:S(2)}) copy-start(bf16[128,1024]{1,0:T(8,128)(2,1)} %param.13) | copy-start | bytes 786436
  147.2 49.7 %all-to-all-start.3 = ((f32[4,8,128]{2,1,0:T(8,128)}), f32[4,8,128]{2,1,0:T(8,128)S(1)}, u32[]{:S(2)}, u32[]{:S(2)}) async-start(f32[4,8,128]{2,1,0:T(8,128)} %bitcast.46), calls=%async_computation.5 | async-start | bytes 32768 | tf_op jit(solution)/shard_map/all_to_all | solution.py:113
  153.4 96.6 %reduce-scatter.5.cloned.1.call-start = ((), (), s32[]{:S(2)}) async-start(), calls=%async_computation.9 | async-start | bytes 1310720 | tf_op jit(solution)/shard_map/reduce_scatter | solution.py:150
  194.1 2.8 %copy-start.1 = (f32[2,1024,128]{2,1,0:T(8,128)S(1)}, f32[2,1024,128]{2,1,0:T(8,128)}, u32[]{:S(2)}) copy-start(f32[2,1024,128]{2,1,0:T(8,128)} %custom-call.1) | copy-start | bytes 3145732
  194.2 2.8 %copy-start.2 = (bf16[2,1024,128]{2,1,0:T(8,128)(2,1)S(1)}, bf16[2,1024,128]{2,1,0:T(8,128)(2,1)}, u32[]{:S(2)}) copy-start(bf16[2,1024,128]{2,1,0:T(8,128)(2,1)} %copy.98) | copy-start | bytes 1572868
  198.7 2.0 copy-start
  211.7 2.0 copy-start
  224.5 2.0 copy-start
  237.3 2.0 copy-start
Sparse Core Ops, SparseCore 0:
  10.1 18.0 all-gather.2
  30.3 16.7 all-gather.4
  101.8 27.7 reduce-scatter.2
  197.0 25.6 reduce-scatter.4
where the time goes:
time: 262 us; the launch traced here: 257 us
  matrix products  98.4 us (38%)
  local copies, waits for them, and re-layouts  48.4 us (18%)
  blocking collectives  32.7 us (12%)
  waiting for transfers between devices  25.4 us (10%)
  starting transfers between devices  21.1 us (8%)
  other arithmetic  16.5 us (6%)
  between operations  13.9 us (5%)
    dot_general x20, matrix products, logits_of(): jnp.einsum('grd,kd->grk', query_part, key_part, preferred_element_type=jn...  30.2 us
    dot_general x4, matrix products, kv_from(): jnp.einsum('grk,grd->kd', grad_logit, query_part, preferred_element_type=...  20.9 us
    dot_general x8, matrix products, query_only(): jnp.einsum('grk,kd->grd', grad_logit, inputs[4], preferred_element_type=j...  20.7 us
    dot_general x8, matrix products, block_forward_pass(): jnp.einsum('grk,kd->grd', exponent_terms.astype(jnp.bfloat16), value_port...  17.5 us
    all_to_all x1, waiting for transfers between devices, per_device(): lax.all_to_all(query_rows, 'qry', split_axis=1, concat_axis=0, tiled=True)  14.7 us
    unnamed x17, local copies, waits for them, and re-layouts  14.6 us
    psum x1, blocking collectives, per_device(): totals = lax.psum(local_sum * weight, 'key')  10.2 us
    pmax x1, blocking collectives, per_device(): peak = lax.pmax(local_peak, 'key')  9.44 us
  transfers between devices with their start and end apart: 7, of which 3 were waited for; matrix products, arithmetic and copies ran while one was open for 60% of the time, Pallas kernels for 0%

commit v1 on v0

v1 whole, which is shorter than its diff:
```python
import functools
import math

import jax
import jax.numpy as jnp
from jax import lax
from jax.experimental import pallas as pl
from jax.experimental.pallas import tpu as pltpu
from jax.sharding import PartitionSpec as P

HQ = 32
KVH = 8
HD = 128
MESH = pl.DeviceIdType.MESH
F32 = jnp.float32
BF16 = jnp.bfloat16


def nt(a, b):
    return lax.dot_general(a, b, (((1,), (1,)), ((), ())), preferred_element_type=F32)


def nn(a, b):
    return lax.dot_general(a, b, (((1,), (0,)), ((), ())), preferred_element_type=F32)


def kernel(
    n_key, n_qry,
    q_ref, d_ref, k_hbm, v_hbm,
    attn_ref, dq_ref, dk_ref, dv_ref,
    qg, dg, ks, vs, kt, vt, exps, part, stat, part_in, stat_in, norm, norm_in,
    dqp, dqp_in, dk_acc, dv_acc,
    kv_sem, q_s, q_r, d_s, d_r, o_s, o_r, st_s, st_r, n_s, n_r, dq_s, dq_r,
):
    factor = 1.0 / math.sqrt(HD)
    log2e_factor = factor * math.log2(math.e)
    per_group = HQ // KVH
    r = n_key // n_qry
    nb = n_key
    rows, cols = q_ref.shape
    heads = cols // HD
    chunk = min(per_group, heads)
    ng = heads // chunk
    kv_cols = ks.shape[1]
    me_c = lax.axis_index("ckpt")
    me_k = lax.axis_index("key")
    me_q = lax.axis_index("qry")
    plane = me_k // r
    my_block = me_q * r + me_k % r
    my_step = (me_q - plane + n_qry) % n_qry

    kv_off = pl.ds(pl.multiple_of(me_q * kv_cols, HD), kv_cols)
    k_copy = pltpu.make_async_copy(k_hbm.at[:, kv_off], ks, kv_sem.at[0])
    v_copy = pltpu.make_async_copy(v_hbm.at[:, kv_off], vs, kv_sem.at[1])
    k_copy.start()
    v_copy.start()

    def is_me(k, q):
        return jnp.logical_and(me_k == k, me_q == q)

    def other(k, q):
        return jnp.logical_or(me_k != k, me_q != q)

    targets = [(k, plane) for k in range(n_key)]
    sources = [(me_q * r + j, q) for q in range(n_qry) for j in range(r)]
    barrier = pltpu.get_barrier_semaphore()
    for k, q in targets + sources:
        @pl.when(other(k, q))
        def _():
            pl.semaphore_signal(barrier, inc=1, device_id=(me_c, k, q), device_id_type=MESH)

    @pl.when(plane == me_q)
    def _():
        pl.semaphore_wait(barrier, 2 * n_key - 2)

    @pl.when(plane != me_q)
    def _():
        pl.semaphore_wait(barrier, 2 * n_key)

    def send(src, dst, ssem, rsem, k, q):
        @pl.when(is_me(k, q))
        def _():
            pltpu.make_async_copy(src, dst, rsem).start()

        @pl.when(other(k, q))
        def _():
            pltpu.make_async_remote_copy(
                src, dst, ssem, rsem, device_id=(me_c, k, q), device_id_type=MESH
            ).start()

    def sent(src, dst, ssem, rsem, k, q):
        @pl.when(other(k, q))
        def _():
            pltpu.make_async_remote_copy(
                src, dst, ssem, rsem, device_id=(me_c, k, q), device_id_type=MESH
            ).wait_send()

    def arrived(dst, rsem):
        pltpu.make_async_copy(dst, dst, rsem).wait()

    q_args = [
        (q_ref, qg.at[my_block], q_s.at[i], q_r.at[my_block], k, q)
        for i, (k, q) in enumerate(targets)
    ]
    d_args = [
        (d_ref, dg.at[my_block], d_s.at[i], d_r.at[my_block], k, q)
        for i, (k, q) in enumerate(targets)
    ]
    for args in q_args:
        send(*args)
    for args in d_args:
        send(*args)

    dk_acc[...] = jnp.zeros_like(dk_acc)
    dv_acc[...] = jnp.zeros_like(dv_acc)
    k_copy.wait()
    v_copy.wait()
    for g in range(kv_cols // HD):
        at = slice(g * HD, (g + 1) * HD)
        kt[at, :] = ks[:, at].astype(F32).T.astype(BF16)
        vt[at, :] = vs[:, at].astype(F32).T.astype(BF16)

    def stacked(ref, b, gi):
        return jnp.concatenate(
            [ref[b, :, (gi * chunk + c) * HD : (gi * chunk + c + 1) * HD] for c in range(chunk)],
            axis=0,
        )

    def o_args(b, j, qq):
        k, q = me_q * r + j, qq
        return (
            (part.at[b], part_in.at[me_k], o_s.at[b], o_r.at[me_k], k, q),
            (stat.at[b], stat_in.at[me_k], st_s.at[b], st_r.at[me_k], k, q),
            (dqp.at[b], dqp_in.at[me_k], dq_s.at[b], dq_r.at[me_k], k, q),
        )

    n_args = [
        (norm, norm_in.at[my_block], n_s.at[i], n_r.at[my_block], k, q)
        for i, (k, q) in enumerate(targets)
    ]

    def forward(b, j):
        arrived(qg.at[b], q_r.at[b])
        for gi in range(ng):
            kv = (j * heads + gi * chunk) // per_group
            at = slice(kv * HD, (kv + 1) * HD)
            scores = nt(ks[:, at], stacked(qg, b, gi))
            top = jnp.max(scores, axis=0, keepdims=True)
            terms = jnp.exp2(scores * log2e_factor - top * log2e_factor)
            total = jnp.sum(terms, axis=0, keepdims=True)
            small = terms.astype(BF16)
            exps[b, gi] = small
            out = nn(vt[at, :], small)
            for c in range(chunk):
                h = gi * chunk + c
                lanes = slice(c * rows, (c + 1) * rows)
                part[b, h * HD : (h + 1) * HD, :] = out[:, lanes].astype(BF16)
                stat[b, h : h + 1, :] = top[:, lanes] * factor
                stat[b, heads + h : heads + h + 1, :] = total[:, lanes]

    def combine():
        for k in range(n_key):
            arrived(part_in.at[k], o_r.at[k])
            arrived(stat_in.at[k], st_r.at[k])
        for h in range(heads):
            at = slice(h * HD, (h + 1) * HD)
            peaks = [stat_in[k, h : h + 1, :] for k in range(n_key)]
            peak = functools.reduce(jnp.maximum, peaks)
            weights = [jnp.exp(p - peak) for p in peaks]
            total = sum(w * stat_in[k, heads + h : heads + h + 1, :] for k, w in enumerate(weights))
            out = sum(w * part_in[k, at, :].astype(F32) for k, w in enumerate(weights)) / total
            attn = out.T.astype(BF16)
            attn_ref[:, at] = attn
            product = d_ref[:, at].astype(F32) * attn.astype(F32)
            norm[h : h + 1, :] = peak + jnp.log(total)
            norm[heads + h : heads + h + 1, :] = jnp.sum(product.T, axis=0, keepdims=True)
        for args in n_args:
            send(*args)

    def backward(b, j):
        arrived(norm_in.at[b], n_r.at[b])
        arrived(dg.at[b], d_r.at[b])
        for gi in range(ng):
            kv = (j * heads + gi * chunk) // per_group
            at = slice(kv * HD, (kv + 1) * HD)
            queries = stacked(qg, b, gi)
            grads = stacked(dg, b, gi)
            hs = [gi * chunk + c for c in range(chunk)]
            scale = jnp.concatenate(
                [jnp.exp(stat[b, h : h + 1, :] - norm_in[b, h : h + 1, :]) for h in hs], axis=1
            )
            delta = jnp.concatenate(
                [norm_in[b, heads + h : heads + h + 1, :] for h in hs], axis=1
            )
            probs = exps[b, gi].astype(F32) * scale
            grad_prob = nt(vs[:, at], grads)
            grad_logit = (probs * (grad_prob - delta)).astype(BF16)
            dv_acc[:, at] += nn(probs.astype(BF16), grads)
            dk_acc[:, at] += nn(grad_logit, queries)
            dq = nn(kt[at, :], grad_logit)
            for c in range(chunk):
                h = gi * chunk + c
                dqp[b, h * HD : (h + 1) * HD, :] = dq[:, c * rows : (c + 1) * rows].astype(BF16)

    @pl.loop(0, n_qry)
    def _(s):
        qq = (me_q + s) % n_qry
        for j in range(r):
            b = qq * r + j
            forward(b, j)
            o, st, _ = o_args(b, j, qq)
            send(*o)
            send(*st)

        @pl.when(jnp.logical_and(s > 0, my_step == s - 1))
        def _():
            combine()

    @pl.when(my_step == n_qry - 1)
    def _():
        combine()

    @pl.loop(0, n_qry)
    def _(s):
        qq = (me_q + s) % n_qry
        for j in range(r):
            b = qq * r + j
            backward(b, j)
            send(*o_args(b, j, qq)[2])

    dk_ref[...] = (dk_acc[...] * factor).astype(BF16)
    dv_ref[...] = dv_acc[...].astype(BF16)
    for k in range(n_key):
        arrived(dqp_in.at[k], dq_r.at[k])
    for h in range(heads):
        at = slice(h * HD, (h + 1) * HD)
        total = sum(dqp_in[k, at, :].astype(F32) for k in range(n_key))
        dq_ref[:, at] = (total.T * factor).astype(BF16)

    for args in q_args + d_args + n_args:
        sent(*args)
    for q in range(n_qry):
        for j in range(r):
            for args in o_args(q * r + j, j, q):
                sent(*args)


def per_device(n_key, n_qry, queries, keys, values, out_grad):
    rows, cols = queries.shape
    key_count = keys.shape[0]
    kv_cols = keys.shape[1] // n_qry
    heads = cols // HD
    chunk = min(HQ // KVH, heads)
    ng = heads // chunk
    vmem = pl.BlockSpec(memory_space=pltpu.VMEM)
    hbm = pl.BlockSpec(memory_space=pl.ANY)
    dma = pltpu.SemaphoreType.DMA
    sems = [dma((2,))] + [dma((n_key,)) for _ in range(12)]
    return pl.pallas_call(
        functools.partial(kernel, n_key, n_qry),
        out_shape=(
            jax.ShapeDtypeStruct((rows, cols), BF16),
            jax.ShapeDtypeStruct((rows, cols), BF16),
            jax.ShapeDtypeStruct((key_count, kv_cols), BF16),
            jax.ShapeDtypeStruct((key_count, kv_cols), BF16),
        ),
        in_specs=[vmem, vmem, hbm, hbm],
        out_specs=(vmem, vmem, vmem, vmem),
        scratch_shapes=[
            pltpu.VMEM((n_key, rows, cols), BF16),
            pltpu.VMEM((n_key, rows, cols), BF16),
            pltpu.VMEM((key_count, kv_cols), BF16),
            pltpu.VMEM((key_count, kv_cols), BF16),
            pltpu.VMEM((kv_cols, key_count), BF16),
            pltpu.VMEM((kv_cols, key_count), BF16),
            pltpu.VMEM((n_key, ng, key_count, chunk * rows), BF16),
            pltpu.VMEM((n_key, cols, rows), BF16),
            pltpu.VMEM((n_key, 2 * heads, rows), F32),
            pltpu.VMEM((n_key, cols, rows), BF16),
            pltpu.VMEM((n_key, 2 * heads, rows), F32),
            pltpu.VMEM((2 * heads, rows), F32),
            pltpu.VMEM((n_key, 2 * heads, rows), F32),
            pltpu.VMEM((n_key, cols, rows), BF16),
            pltpu.VMEM((n_key, cols, rows), BF16),
            pltpu.VMEM((key_count, kv_cols), F32),
            pltpu.VMEM((key_count, kv_cols), F32),
        ]
        + sems,
        compiler_params=pltpu.CompilerParams(
            collective_id=0, has_side_effects=True, vmem_limit_bytes=60 * 1024 * 1024
        ),
        name="attention",
    )(queries, out_grad, keys, values)


def solution(mesh):
    spec_q = P(("ckpt", "qry"), "key")
    spec_k = P(("ckpt", "key"), None)
    spec_o = P(("ckpt", "key"), "qry")
    body = functools.partial(per_device, mesh.shape["key"], mesh.shape["qry"])
    return jax.shard_map(
        body,
        mesh=mesh,
        in_specs=(spec_q, spec_k, spec_k, spec_q),
        out_specs=(spec_q, spec_q, spec_o, spec_o),
        check_vma=False,
    )
```

time: 262 us -> 155 us (0.59); the launches traced: 257 us -> 155 us
  Pallas kernels: 0 us -> 149 us
  matrix products: 98.4 us -> 0 us
  local copies, waits for them, and re-layouts: 48.4 us -> 6.06 us
  blocking collectives: 32.7 us -> 0 us
  waiting for transfers between devices: 25.4 us -> 0 us
  starting transfers between devices: 21.1 us -> 0 us
  other arithmetic: 16.5 us -> 0 us
  between operations: 13.9 us -> 0.65 us
    pallas_call x0 -> x1, Pallas kernels: none -> 149 us  [per_device(): pl.pallas_call(functools.partial(kernel, n_key, n_qry), out_shape=(jax.Sh...]
    dot_general x44 -> x0, matrix products: 98.4 us -> none  [the longest x20 30.2 us: logits_of(): jnp.einsum('grd,kd->grk', query_part, key_part, preferred_element_type=jn...]
    all_to_all x3 -> x0, waiting for transfers between devices: 21.2 us -> none  [the longest x1 14.7 us: per_device(): lax.all_to_all(query_rows, 'qry', split_axis=1, concat_axis=0, tiled=True)]
    all_to_all x3 -> x0, starting transfers between devices: 21 us -> none  [the longest x1 8.4 us: per_device(): lax.all_to_all(grad_rows, 'qry', split_axis=1, concat_axis=0, tiled=True)]
    while x11 -> x0, local copies, waits for them, and re-layouts: 15.8 us -> none
    psum x1 -> x0, blocking collectives: 10.2 us -> none  [per_device(): totals = lax.psum(local_sum * weight, 'key')]
    convert_element_type x4 -> x0, local copies, waits for them, and re-layouts: 10.1 us -> none  [the longest x2 5.76 us: per_device(): query_flat.astype(jnp.bfloat16)]
    pmax x1 -> x0, blocking collectives: 9.44 us -> none  [per_device(): peak = lax.pmax(local_peak, 'key')]
  transfers between devices with their start and end apart: 7 -> 0, of which waited for: 3 -> 0; matrix products, arithmetic and copies ran while one was open for 60% -> 0% of each run, Pallas kernels for 0% -> 0%
where the time goes in v1:
time: 155 us
  Pallas kernels  149 us (96%)
  local copies, waits for them, and re-layouts  6.06 us (4%)
    pallas_call x1, Pallas kernels, per_device(): pl.pallas_call(functools.partial(kernel, n_key, n_qry), out_shape=(jax.Sh...  149 us
    unnamed x6, local copies, waits for them, and re-layouts  6.06 us

profile of v1, /device:TPU:29, one launch (start us, length us, event | category | flops | bytes accessed | tf_op | source)
XLA Modules:
  0.0 155.2 jit_solution(13985970562496150150)
XLA Ops:
  0.6 148.5 %attention.1 = (bf16[128,1024]{1,0:T(8,128)(2,1)}, bf16[128,1024]{1,0:T(8,128)(2,1)}, bf16[1024,256]{1,0:T(8,128)(2,1)}, bf16[1024,256]{1,0:T(8,128)(2,1)}) custom-call(bf16[128,1024]{1,0:T(8,128)(2,1)} %q_ref.1, bf16[128,1024]{1,0:T(8,128)(2,1)} %d_ref.1, bf16[1024,1024]{1,0:T(8,128)(2,1)} %k_hbm.1, bf16[1024,1024]{1,0:T(8,128)(2,1)} %v_hbm.1), custom_call_target="tpu_custom_call" | custom-call | tf_op jit(solution)/shard_map/attention/pallas_call | solution.py:259
  149.2 0.0 copy-start
  149.2 1.7 %copy.12 = bf16[128,1024]{1,0:T(8,128)(2,1)} copy(bf16[128,1024]{1,0:T(8,128)(2,1)} %get-tuple-element.8) | data formatting | bytes 524288
  150.9 1.7 %copy.13 = bf16[128,1024]{1,0:T(8,128)(2,1)} copy(bf16[128,1024]{1,0:T(8,128)(2,1)} %get-tuple-element.9) | data formatting | bytes 524288
  152.6 1.9 %copy.14 = bf16[1024,256]{1,0:T(8,128)(2,1)} copy(bf16[1024,256]{1,0:T(8,128)(2,1)} %get-tuple-element.10) | data formatting | bytes 1048576
  154.4 0.0 copy-done
  154.4 0.8 copy.15
Async XLA Ops:
  149.2 5.3 %copy-start = (bf16[1024,256]{1,0:T(8,128)(2,1)S(1)}, bf16[1024,256]{1,0:T(8,128)(2,1)}, u32[]{:S(2)}) copy-start(bf16[1024,256]{1,0:T(8,128)(2,1)} %get-tuple-element.11) | copy-start | bytes 1572868

commit v2 on v1

--- a/solution.py
+++ b/solution.py
@@ -25,12 +25,12 @@
 
 
 def kernel(
-    n_key, n_qry,
+    n_key, n_qry, split,
     q_ref, d_ref, k_hbm, v_hbm,
     attn_ref, dq_ref, dk_ref, dv_ref,
     qg, dg, ks, vs, kt, vt, exps, part, stat, part_in, stat_in, norm, norm_in,
-    dqp, dqp_in, dk_acc, dv_acc,
-    kv_sem, q_s, q_r, d_s, d_r, o_s, o_r, st_s, st_r, n_s, n_r, dq_s, dq_r,
+    dqp, dqp_in, dk_acc, dv_acc, dkv, dkv_in,
+    kv_sem, kx_s, kx_r, gx_s, gx_r, q_s, q_r, d_s, d_r, o_s, o_r, st_s, st_r, n_s, n_r, dq_s, dq_r,
 ):
     factor = 1.0 / math.sqrt(HD)
     log2e_factor = factor * math.log2(math.e)
@@ -38,10 +38,13 @@
     r = n_key // n_qry
     nb = n_key
     rows, cols = q_ref.shape
-    heads = cols // HD
+    all_heads = cols // HD
+    heads = all_heads // split
+    wide = heads * HD
     chunk = min(per_group, heads)
     ng = heads // chunk
     kv_cols = ks.shape[1]
+    key_count = k_hbm.shape[0]
     me_c = lax.axis_index("ckpt")
     me_k = lax.axis_index("key")
     me_q = lax.axis_index("qry")
@@ -49,9 +52,16 @@
     my_block = me_q * r + me_k % r
     my_step = (me_q - plane + n_qry) % n_qry
 
-    kv_off = pl.ds(pl.multiple_of(me_q * kv_cols, HD), kv_cols)
-    k_copy = pltpu.make_async_copy(k_hbm.at[:, kv_off], ks, kv_sem.at[0])
-    v_copy = pltpu.make_async_copy(v_hbm.at[:, kv_off], vs, kv_sem.at[1])
+    core = me_k % split
+    partner = me_k + (split - 1) - 2 * core
+
+    def head_part(c):
+        start = (me_q * split + c) * kv_cols
+        return pl.ds(pl.multiple_of(start, HD), kv_cols)
+
+    own_rows = pl.ds(pl.multiple_of(core * key_count, HD), key_count)
+    k_copy = pltpu.make_async_copy(k_hbm.at[:, head_part(core)], ks.at[own_rows], kv_sem.at[0])
+    v_copy = pltpu.make_async_copy(v_hbm.at[:, head_part(core)], vs.at[own_rows], kv_sem.at[1])
     k_copy.start()
     v_copy.start()
 
@@ -69,13 +79,16 @@
         def _():
             pl.semaphore_signal(barrier, inc=1, device_id=(me_c, k, q), device_id_type=MESH)
 
+    if split > 1:
+        pl.semaphore_signal(barrier, inc=1, device_id=(me_c, partner, me_q), device_id_type=MESH)
+
     @pl.when(plane == me_q)
     def _():
-        pl.semaphore_wait(barrier, 2 * n_key - 2)
+        pl.semaphore_wait(barrier, 2 * n_key - 2 + (split - 1))
 
     @pl.when(plane != me_q)
     def _():
-        pl.semaphore_wait(barrier, 2 * n_key)
+        pl.semaphore_wait(barrier, 2 * n_key + (split - 1))
 
     def send(src, dst, ssem, rsem, k, q):
         @pl.when(is_me(k, q))
@@ -98,16 +111,32 @@
     def arrived(dst, rsem):
         pltpu.make_async_copy(dst, dst, rsem).wait()
 
+    def half(k):
+        return slice((k % split) * wide, (k % split + 1) * wide)
+
+    def to_partner(src, dst, i, ssem, rsem):
+        return pltpu.make_async_remote_copy(
+            src, dst, ssem.at[i], rsem.at[i],
+            device_id=(me_c, partner, me_q), device_id_type=MESH,
+        )
+
     q_args = [
-        (q_ref, qg.at[my_block], q_s.at[i], q_r.at[my_block], k, q)
+        (q_ref.at[:, half(k)], qg.at[my_block], q_s.at[i], q_r.at[my_block], k, q)
         for i, (k, q) in enumerate(targets)
     ]
     d_args = [
-        (d_ref, dg.at[my_block], d_s.at[i], d_r.at[my_block], k, q)
+        (d_ref.at[:, half(k)], dg.at[my_block], d_s.at[i], d_r.at[my_block], k, q)
         for i, (k, q) in enumerate(targets)
     ]
     for args in q_args:
         send(*args)
+    if split > 1:
+        kv_moves = [
+            to_partner(src.at[:, head_part(1 - core)], dst.at[own_rows], i, kx_s, kx_r)
+            for i, (src, dst) in enumerate(((k_hbm, ks), (v_hbm, vs)))
+        ]
+        for move in kv_moves:
+            move.start()
     for args in d_args:
         send(*args)
 
@@ -115,6 +144,9 @@
     dv_acc[...] = jnp.zeros_like(dv_acc)
     k_copy.wait()
     v_copy.wait()
+    if split > 1:
+        for move in kv_moves:
+            move.wait_recv()
     for g in range(kv_cols // HD):
         at = slice(g * HD, (g + 1) * HD)
         kt[at, :] = ks[:, at].astype(F32).T.astype(BF16)
@@ -135,7 +167,7 @@
         )
 
     n_args = [
-        (norm, norm_in.at[my_block], n_s.at[i], n_r.at[my_block], k, q)
+        (norm.at[k % split], norm_in.at[my_block], n_s.at[i], n_r.at[my_block], k, q)
         for i, (k, q) in enumerate(targets)
     ]
 
@@ -162,18 +194,23 @@
         for k in range(n_key):
             arrived(part_in.at[k], o_r.at[k])
             arrived(stat_in.at[k], st_r.at[k])
-        for h in range(heads):
+        for h in range(all_heads):
             at = slice(h * HD, (h + 1) * HD)
-            peaks = [stat_in[k, h : h + 1, :] for k in range(n_key)]
+            c, w = h // heads, h % heads
+            block = slice(w * HD, (w + 1) * HD)
+            members = range(c, n_key, split)
+            peaks = [stat_in[k, w : w + 1, :] for k in members]
             peak = functools.reduce(jnp.maximum, peaks)
             weights = [jnp.exp(p - peak) for p in peaks]
-            total = sum(w * stat_in[k, heads + h : heads + h + 1, :] for k, w in enumerate(weights))
-            out = sum(w * part_in[k, at, :].astype(F32) for k, w in enumerate(weights)) / total
-            attn = out.T.astype(BF16)
+            total = sum(
+                x * stat_in[k, heads + w : heads + w + 1, :] for k, x in zip(members, weights)
+            )
+            out = sum(x * part_in[k, block, :].astype(F32) for k, x in zip(members, weights))
+            attn = (out / total).T.astype(BF16)
             attn_ref[:, at] = attn
             product = d_ref[:, at].astype(F32) * attn.astype(F32)
-            norm[h : h + 1, :] = peak + jnp.log(total)
-            norm[heads + h : heads + h + 1, :] = jnp.sum(product.T, axis=0, keepdims=True)
+            norm[c, w : w + 1, :] = peak + jnp.log(total)
+            norm[c, heads + w : heads + w + 1, :] = jnp.sum(product.T, axis=0, keepdims=True)
         for args in n_args:
             send(*args)
 
@@ -228,15 +265,44 @@
             backward(b, j)
             send(*o_args(b, j, qq)[2])
 
-    dk_ref[...] = (dk_acc[...] * factor).astype(BF16)
-    dv_ref[...] = dv_acc[...].astype(BF16)
+    if split > 1:
+        other_rows = pl.ds(pl.multiple_of((1 - core) * key_count, HD), key_count)
+        dkv[0] = (dk_acc[other_rows, :] * factor).astype(BF16)
+        dkv[1] = dv_acc[other_rows, :].astype(BF16)
+        grad_moves = [to_partner(dkv.at[i], dkv_in.at[i], i, gx_s, gx_r) for i in range(2)]
+        for move in grad_moves:
+            move.start()
+        for c in range(split):
+            mine = slice(c * kv_cols, (c + 1) * kv_cols)
+
+            @pl.when(core == c)
+            def _():
+                dk_ref[:, mine] = (dk_acc[own_rows, :] * factor).astype(BF16)
+                dv_ref[:, mine] = dv_acc[own_rows, :].astype(BF16)
+        for move in grad_moves:
+            move.wait_recv()
+        for c in range(split):
+            theirs = slice((1 - c) * kv_cols, (2 - c) * kv_cols)
+
+            @pl.when(core == c)
+            def _():
+                dk_ref[:, theirs] = dkv_in[0]
+                dv_ref[:, theirs] = dkv_in[1]
+    else:
+        dk_ref[...] = (dk_acc[...] * factor).astype(BF16)
+        dv_ref[...] = dv_acc[...].astype(BF16)
     for k in range(n_key):
         arrived(dqp_in.at[k], dq_r.at[k])
-    for h in range(heads):
+    for h in range(all_heads):
         at = slice(h * HD, (h + 1) * HD)
-        total = sum(dqp_in[k, at, :].astype(F32) for k in range(n_key))
+        c, w = h // heads, h % heads
+        block = slice(w * HD, (w + 1) * HD)
+        total = sum(dqp_in[k, block, :].astype(F32) for k in range(c, n_key, split))
         dq_ref[:, at] = (total.T * factor).astype(BF16)
 
+    if split > 1:
+        for move in kv_moves + grad_moves:
+            move.wait_send()
     for args in q_args + d_args + n_args:
         sent(*args)
     for q in range(n_qry):
@@ -249,15 +315,19 @@
     rows, cols = queries.shape
     key_count = keys.shape[0]
     kv_cols = keys.shape[1] // n_qry
-    heads = cols // HD
+    split = 2 if n_key == n_qry and (kv_cols // HD) % 2 == 0 else 1
+    heads = cols // HD // split
+    wide = heads * HD
     chunk = min(HQ // KVH, heads)
     ng = heads // chunk
+    kv_wide = kv_cols // split
+    key_rows = key_count * split
     vmem = pl.BlockSpec(memory_space=pltpu.VMEM)
     hbm = pl.BlockSpec(memory_space=pl.ANY)
     dma = pltpu.SemaphoreType.DMA
-    sems = [dma((2,))] + [dma((n_key,)) for _ in range(12)]
+    sems = [dma((2,))] + [dma((2,)) for _ in range(4)] + [dma((n_key,)) for _ in range(12)]
     return pl.pallas_call(
-        functools.partial(kernel, n_key, n_qry),
+        functools.partial(kernel, n_key, n_qry, split),
         out_shape=(
             jax.ShapeDtypeStruct((rows, cols), BF16),
             jax.ShapeDtypeStruct((rows, cols), BF16),
@@ -267,23 +337,25 @@
         in_specs=[vmem, vmem, hbm, hbm],
         out_specs=(vmem, vmem, vmem, vmem),
         scratch_shapes=[
-            pltpu.VMEM((n_key, rows, cols), BF16),
-            pltpu.VMEM((n_key, rows, cols), BF16),
-            pltpu.VMEM((key_count, kv_cols), BF16),
-            pltpu.VMEM((key_count, kv_cols), BF16),
-            pltpu.VMEM((kv_cols, key_count), BF16),
-            pltpu.VMEM((kv_cols, key_count), BF16),
-            pltpu.VMEM((n_key, ng, key_count, chunk * rows), BF16),
-            pltpu.VMEM((n_key, cols, rows), BF16),
+            pltpu.VMEM((n_key, rows, wide), BF16),
+            pltpu.VMEM((n_key, rows, wide), BF16),
+            pltpu.VMEM((key_rows, kv_wide), BF16),
+            pltpu.VMEM((key_rows, kv_wide), BF16),
+            pltpu.VMEM((kv_wide, key_rows), BF16),
+            pltpu.VMEM((kv_wide, key_rows), BF16),
+            pltpu.VMEM((n_key, ng, key_rows, chunk * rows), BF16),
+            pltpu.VMEM((n_key, wide, rows), BF16),
             pltpu.VMEM((n_key, 2 * heads, rows), F32),
-            pltpu.VMEM((n_key, cols, rows), BF16),
+            pltpu.VMEM((n_key, wide, rows), BF16),
             pltpu.VMEM((n_key, 2 * heads, rows), F32),
-            pltpu.VMEM((2 * heads, rows), F32),
+            pltpu.VMEM((split, 2 * heads, rows), F32),
             pltpu.VMEM((n_key, 2 * heads, rows), F32),
-            pltpu.VMEM((n_key, cols, rows), BF16),
-            pltpu.VMEM((n_key, cols, rows), BF16),
-            pltpu.VMEM((key_count, kv_cols), F32),
-            pltpu.VMEM((key_count, kv_cols), F32),
+            pltpu.VMEM((n_key, wide, rows), BF16),
+            pltpu.VMEM((n_key, wide, rows), BF16),
+            pltpu.VMEM((key_rows, kv_wide), F32),
+            pltpu.VMEM((key_rows, kv_wide), F32),
+            pltpu.VMEM((2, key_count, kv_wide), BF16),
+            pltpu.VMEM((2, key_count, kv_wide), BF16),
         ]
         + sems,
         compiler_params=pltpu.CompilerParams(

time: 155 us -> 91.6 us (0.59)
  the two profiles are of different devices: /device:TPU:29 before, /device:TPU:1 now
where the time goes in v2:
time: 91.6 us; the launch traced here: 91.3 us
  Pallas kernels  84.6 us (92%)
  local copies, waits for them, and re-layouts  6.06 us (7%)
    pallas_call x1, Pallas kernels, per_device(): pl.pallas_call(functools.partial(kernel, n_key, n_qry, split), out_shape=...  84.6 us
    unnamed x6, local copies, waits for them, and re-layouts  6.06 us

profile of v2, /device:TPU:1, one launch (start us, length us, event | category | flops | bytes accessed | tf_op | source)
XLA Modules:
  0.0 91.3 jit_solution(12123422411046419620)
XLA Ops:
  0.6 84.6 %attention.1 = (bf16[128,1024]{1,0:T(8,128)(2,1)}, bf16[128,1024]{1,0:T(8,128)(2,1)}, bf16[1024,256]{1,0:T(8,128)(2,1)}, bf16[1024,256]{1,0:T(8,128)(2,1)}) custom-call(bf16[128,1024]{1,0:T(8,128)(2,1)} %q_ref.1, bf16[128,1024]{1,0:T(8,128)(2,1)} %d_ref.1, bf16[1024,1024]{1,0:T(8,128)(2,1)} %k_hbm.1, bf16[1024,1024]{1,0:T(8,128)(2,1)} %v_hbm.1), custom_call_target="tpu_custom_call" | custom-call | tf_op jit(solution)/shard_map/attention/pallas_call | solution.py:329
  85.3 0.0 copy-start
  85.3 1.7 %copy.12 = bf16[128,1024]{1,0:T(8,128)(2,1)} copy(bf16[128,1024]{1,0:T(8,128)(2,1)} %get-tuple-element.8) | data formatting | bytes 524288
  87.0 1.7 %copy.13 = bf16[128,1024]{1,0:T(8,128)(2,1)} copy(bf16[128,1024]{1,0:T(8,128)(2,1)} %get-tuple-element.9) | data formatting | bytes 524288
  88.7 1.9 %copy.14 = bf16[1024,256]{1,0:T(8,128)(2,1)} copy(bf16[1024,256]{1,0:T(8,128)(2,1)} %get-tuple-element.10) | data formatting | bytes 1048576
  90.5 0.0 copy-done
  90.5 0.8 copy.15
Async XLA Ops:
  85.3 5.3 %copy-start = (bf16[1024,256]{1,0:T(8,128)(2,1)S(1)}, bf16[1024,256]{1,0:T(8,128)(2,1)}, u32[]{:S(2)}) copy-start(bf16[1024,256]{1,0:T(8,128)(2,1)} %get-tuple-element.11) | copy-start | bytes 1572868

commit v3 on v2

--- a/solution.py
+++ b/solution.py
@@ -25,12 +25,12 @@
 
 
 def kernel(
-    n_key, n_qry, split,
+    n_key, n_qry, split, relay,
     q_ref, d_ref, k_hbm, v_hbm,
     attn_ref, dq_ref, dk_ref, dv_ref,
     qg, dg, ks, vs, kt, vt, exps, part, stat, part_in, stat_in, norm, norm_in,
-    dqp, dqp_in, dk_acc, dv_acc, dkv, dkv_in,
-    kv_sem, kx_s, kx_r, gx_s, gx_r, q_s, q_r, d_s, d_r, o_s, o_r, st_s, st_r, n_s, n_r, dq_s, dq_r,
+    dqp, dqp_in, dk_acc, dv_acc, dkv, dkv_in, crossed,
+    kv_sem, kx_s, kx_r, gx_s, gx_r, q_s, q_r, d_s, d_r, o_s, o_r, st_s, st_r, n_s, n_r, dq_s, dq_r, q_xs, q_xr, d_xs, d_xr, x_s, x_r,
 ):
     factor = 1.0 / math.sqrt(HD)
     log2e_factor = factor * math.log2(math.e)
@@ -74,21 +74,32 @@
     targets = [(k, plane) for k in range(n_key)]
     sources = [(me_q * r + j, q) for q in range(n_qry) for j in range(r)]
     barrier = pltpu.get_barrier_semaphore()
-    for k, q in targets + sources:
-        @pl.when(other(k, q))
-        def _():
-            pl.semaphore_signal(barrier, inc=1, device_id=(me_c, k, q), device_id_type=MESH)
-
-    if split > 1:
-        pl.semaphore_signal(barrier, inc=1, device_id=(me_c, partner, me_q), device_id_type=MESH)
-
-    @pl.when(plane == me_q)
-    def _():
-        pl.semaphore_wait(barrier, 2 * n_key - 2 + (split - 1))
-
-    @pl.when(plane != me_q)
-    def _():
-        pl.semaphore_wait(barrier, 2 * n_key + (split - 1))
+    if relay:
+        for k in range(n_key):
+            for q in range(n_qry):
+                @pl.when(other(k, q))
+                def _():
+                    pl.semaphore_signal(
+                        barrier, inc=1, device_id=(me_c, k, q), device_id_type=MESH
+                    )
+
+        pl.semaphore_wait(barrier, n_key * n_qry - 1)
+    else:
+        for k, q in targets + sources:
+            @pl.when(other(k, q))
+            def _():
+                pl.semaphore_signal(barrier, inc=1, device_id=(me_c, k, q), device_id_type=MESH)
+
+        if split > 1:
+            pl.semaphore_signal(barrier, inc=1, device_id=(me_c, partner, me_q), device_id_type=MESH)
+
+        @pl.when(plane == me_q)
+        def _():
+            pl.semaphore_wait(barrier, 2 * n_key - 2 + (split - 1))
+
+        @pl.when(plane != me_q)
+        def _():
+            pl.semaphore_wait(barrier, 2 * n_key + (split - 1))
 
     def send(src, dst, ssem, rsem, k, q):
         @pl.when(is_me(k, q))
@@ -128,17 +139,67 @@
         (d_ref.at[:, half(k)], dg.at[my_block], d_s.at[i], d_r.at[my_block], k, q)
         for i, (k, q) in enumerate(targets)
     ]
-    for args in q_args:
-        send(*args)
     if split > 1:
         kv_moves = [
             to_partner(src.at[:, head_part(1 - core)], dst.at[own_rows], i, kx_s, kx_r)
             for i, (src, dst) in enumerate(((k_hbm, ks), (v_hbm, vs)))
         ]
+    if relay:
+        low = rows // 2
+        chip = me_k // split
+        beside = (1 - chip) * split + core
+        far = (chip + me_q // split) % 2
+        got = pl.ds(pl.multiple_of(far * low, low), low)
+
+        def across(src, dst, ssem, rsem):
+            return pltpu.make_async_remote_copy(
+                src, dst, ssem, rsem, device_id=(me_c, beside, me_q), device_id_type=MESH
+            )
+
+        crossing = [
+            across(ref.at[low:rows], crossed.at[i], x_s.at[i], x_r.at[i])
+            for i, ref in enumerate((q_ref, d_ref))
+        ]
+
+        def along(ref, gathered, ssem, rsem, i):
+            near = [
+                (ref.at[0:low, half(c)], gathered.at[me_q, 0:low], ssem.at[c], rsem.at[me_q],
+                 chip * split + c, me_k)
+                for c in range(split)
+            ]
+            turned = [
+                (crossed.at[i, :, half(c)], gathered.at[me_q, low:rows], ssem.at[split + c],
+                 rsem.at[me_q], chip * split + c, beside)
+                for c in range(split)
+            ]
+            return near, turned
+
+        def passed(gathered, ssem, rsem, b):
+            return across(gathered.at[b, got], gathered.at[b, got], ssem.at[b], rsem.at[b])
+
+        q_near, q_turned = along(q_ref, qg, q_s, q_r, 0)
+        d_near, d_turned = along(d_ref, dg, d_s, d_r, 1)
+        q_args, d_args = q_near + q_turned, d_near + d_turned
+        for move in crossing:
+            move.start()
+        for args in q_near:
+            send(*args)
         for move in kv_moves:
             move.start()
-    for args in d_args:
-        send(*args)
+        crossing[0].wait_recv()
+        for args in q_turned + d_near:
+            send(*args)
+        crossing[1].wait_recv()
+        for args in d_turned:
+            send(*args)
+    else:
+        for args in q_args:
+            send(*args)
+        if split > 1:
+            for move in kv_moves:
+                move.start()
+        for args in d_args:
+            send(*args)
 
     dk_acc[...] = jnp.zeros_like(dk_acc)
     dv_acc[...] = jnp.zeros_like(dv_acc)
@@ -152,6 +213,12 @@
         kt[at, :] = ks[:, at].astype(F32).T.astype(BF16)
         vt[at, :] = vs[:, at].astype(F32).T.astype(BF16)
 
+    if relay:
+        for i in range(n_qry):
+            b = (me_q + i) % n_qry
+            arrived(qg.at[b, got], q_r.at[b])
+            passed(qg, q_xs, q_xr, b).start()
+
     def stacked(ref, b, gi):
         return jnp.concatenate(
             [ref[b, :, (gi * chunk + c) * HD : (gi * chunk + c + 1) * HD] for c in range(chunk)],
@@ -172,7 +239,10 @@
     ]
 
     def forward(b, j):
-        arrived(qg.at[b], q_r.at[b])
+        if relay:
+            passed(qg, q_xs, q_xr, b).wait_recv()
+        else:
+            arrived(qg.at[b], q_r.at[b])
         for gi in range(ng):
             kv = (j * heads + gi * chunk) // per_group
             at = slice(kv * HD, (kv + 1) * HD)
@@ -216,7 +286,10 @@
 
     def backward(b, j):
         arrived(norm_in.at[b], n_r.at[b])
-        arrived(dg.at[b], d_r.at[b])
+        if relay:
+            passed(dg, d_xs, d_xr, b).wait_recv()
+        else:
+            arrived(dg.at[b], d_r.at[b])
         for gi in range(ng):
             kv = (j * heads + gi * chunk) // per_group
             at = slice(kv * HD, (kv + 1) * HD)
@@ -248,6 +321,9 @@
             o, st, _ = o_args(b, j, qq)
             send(*o)
             send(*st)
+            if relay:
+                arrived(dg.at[b, got], d_r.at[b])
+                passed(dg, d_xs, d_xr, b).start()
 
         @pl.when(jnp.logical_and(s > 0, my_step == s - 1))
         def _():
@@ -303,6 +379,12 @@
     if split > 1:
         for move in kv_moves + grad_moves:
             move.wait_send()
+    if relay:
+        for move in crossing:
+            move.wait_send()
+        for b in range(n_qry):
+            passed(qg, q_xs, q_xr, b).wait_send()
+            passed(dg, d_xs, d_xr, b).wait_send()
     for args in q_args + d_args + n_args:
         sent(*args)
     for q in range(n_qry):
@@ -316,6 +398,7 @@
     key_count = keys.shape[0]
     kv_cols = keys.shape[1] // n_qry
     split = 2 if n_key == n_qry and (kv_cols // HD) % 2 == 0 else 1
+    relay = split == 2 and n_key == 2 * split and rows % 32 == 0
     heads = cols // HD // split
     wide = heads * HD
     chunk = min(HQ // KVH, heads)
@@ -325,9 +408,11 @@
     vmem = pl.BlockSpec(memory_space=pltpu.VMEM)
     hbm = pl.BlockSpec(memory_space=pl.ANY)
     dma = pltpu.SemaphoreType.DMA
-    sems = [dma((2,))] + [dma((2,)) for _ in range(4)] + [dma((n_key,)) for _ in range(12)]
+    sems = [dma((2,))] + [dma((2,)) for _ in range(4)] + [dma((n_key,)) for _ in range(16)]
+    sems.append(dma((2,)))
+    sems.append(dma((2,)))
     return pl.pallas_call(
-        functools.partial(kernel, n_key, n_qry, split),
+        functools.partial(kernel, n_key, n_qry, split, relay),
         out_shape=(
             jax.ShapeDtypeStruct((rows, cols), BF16),
             jax.ShapeDtypeStruct((rows, cols), BF16),
@@ -356,6 +441,7 @@
             pltpu.VMEM((key_rows, kv_wide), F32),
             pltpu.VMEM((2, key_count, kv_wide), BF16),
             pltpu.VMEM((2, key_count, kv_wide), BF16),
+            pltpu.VMEM((2, rows // 2, cols), BF16),
         ]
         + sems,
         compiler_params=pltpu.CompilerParams(

time: 91.6 us -> 62.9 us (0.69)
  the two profiles are of different devices: /device:TPU:1 before, /device:TPU:29 now
where the time goes in v3:
time: 62.9 us; the launch traced here: 62.2 us
  Pallas kernels  55.5 us (88%)
  local copies, waits for them, and re-layouts  6.06 us (10%)
  between operations  0.65 us (1%)
    pallas_call x1, Pallas kernels, per_device(): pl.pallas_call(functools.partial(kernel, n_key, n_qry, split, relay), out...  55.5 us
    unnamed x6, local copies, waits for them, and re-layouts  6.06 us

profile of v3, /device:TPU:29, one launch (start us, length us, event | category | flops | bytes accessed | tf_op | source)
XLA Modules:
  0.0 62.2 jit_solution(13966769742225012382)
XLA Ops:
  0.6 55.5 %attention.1 = (bf16[128,1024]{1,0:T(8,128)(2,1)}, bf16[128,1024]{1,0:T(8,128)(2,1)}, bf16[1024,256]{1,0:T(8,128)(2,1)}, bf16[1024,256]{1,0:T(8,128)(2,1)}) custom-call(bf16[128,1024]{1,0:T(8,128)(2,1)} %q_ref.1, bf16[128,1024]{1,0:T(8,128)(2,1)} %d_ref.1, bf16[1024,1024]{1,0:T(8,128)(2,1)} %k_hbm.1, bf16[1024,1024]{1,0:T(8,128)(2,1)} %v_hbm.1), custom_call_target="tpu_custom_call" | custom-call | tf_op jit(solution)/shard_map/attention/pallas_call | solution.py:414
  56.1 0.0 copy-start
  56.1 1.7 %copy.12 = bf16[128,1024]{1,0:T(8,128)(2,1)} copy(bf16[128,1024]{1,0:T(8,128)(2,1)} %get-tuple-element.8) | data formatting | bytes 524288
  57.9 1.7 %copy.13 = bf16[128,1024]{1,0:T(8,128)(2,1)} copy(bf16[128,1024]{1,0:T(8,128)(2,1)} %get-tuple-element.9) | data formatting | bytes 524288
  59.5 1.9 %copy.14 = bf16[1024,256]{1,0:T(8,128)(2,1)} copy(bf16[1024,256]{1,0:T(8,128)(2,1)} %get-tuple-element.10) | data formatting | bytes 1048576
  61.4 0.0 copy-done
  61.4 0.8 %copy.15 = bf16[1024,256]{1,0:T(8,128)(2,1)} copy(bf16[1024,256]{1,0:T(8,128)(2,1)S(1)} %copy-done) | data formatting | bytes 1048576
Async XLA Ops:
  56.1 5.3 %copy-start = (bf16[1024,256]{1,0:T(8,128)(2,1)S(1)}, bf16[1024,256]{1,0:T(8,128)(2,1)}, u32[]{:S(2)}) copy-start(bf16[1024,256]{1,0:T(8,128)(2,1)} %get-tuple-element.11) | copy-start | bytes 1572868

commit v4 on v3

--- a/solution.py
+++ b/solution.py
@@ -213,11 +213,15 @@
         kt[at, :] = ks[:, at].astype(F32).T.astype(BF16)
         vt[at, :] = vs[:, at].astype(F32).T.astype(BF16)
 
+    ahead = min(2, n_qry)
+
+    def pass_queries(b):
+        arrived(qg.at[b, got], q_r.at[b])
+        passed(qg, q_xs, q_xr, b).start()
+
     if relay:
-        for i in range(n_qry):
-            b = (me_q + i) % n_qry
-            arrived(qg.at[b, got], q_r.at[b])
-            passed(qg, q_xs, q_xr, b).start()
+        for i in range(ahead):
+            pass_queries((me_q + i) % n_qry)
 
     def stacked(ref, b, gi):
         return jnp.concatenate(
@@ -322,6 +326,10 @@
             send(*o)
             send(*st)
             if relay:
+                @pl.when(s + ahead < n_qry)
+                def _():
+                    pass_queries((me_q + s + ahead) % n_qry)
+
                 arrived(dg.at[b, got], d_r.at[b])
                 passed(dg, d_xs, d_xr, b).start()
 
@@ -335,7 +343,7 @@
 
     @pl.loop(0, n_qry)
     def _(s):
-        qq = (me_q + s) % n_qry
+        qq = (me_q + s + 1) % n_qry
         for j in range(r):
             b = qq * r + j
             backward(b, j)

time: 62.9 us -> 66 us (1.049)
  the two profiles are of different devices: /device:TPU:29 before, /device:TPU:0 now
where the time goes in v4:
time: 66 us; the launch traced here: 65.7 us
  Pallas kernels  59 us (89%)
  local copies, waits for them, and re-layouts  6.06 us (9%)
    pallas_call x1, Pallas kernels, per_device(): pl.pallas_call(functools.partial(kernel, n_key, n_qry, split, relay), out...  59 us
    unnamed x6, local copies, waits for them, and re-layouts  6.06 us

profile of v4, /device:TPU:0, one launch (start us, length us, event | category | flops | bytes accessed | tf_op | source)
XLA Modules:
  0.0 65.7 jit_solution(14637231883986213553)
XLA Ops:
  0.6 59.0 %attention.1 = (bf16[128,1024]{1,0:T(8,128)(2,1)}, bf16[128,1024]{1,0:T(8,128)(2,1)}, bf16[1024,256]{1,0:T(8,128)(2,1)}, bf16[1024,256]{1,0:T(8,128)(2,1)}) custom-call(bf16[128,1024]{1,0:T(8,128)(2,1)} %q_ref.1, bf16[128,1024]{1,0:T(8,128)(2,1)} %d_ref.1, bf16[1024,1024]{1,0:T(8,128)(2,1)} %k_hbm.1, bf16[1024,1024]{1,0:T(8,128)(2,1)} %v_hbm.1), custom_call_target="tpu_custom_call" | custom-call | tf_op jit(solution)/shard_map/attention/pallas_call | solution.py:422
  59.7 0.0 copy-start
  59.7 1.7 %copy.12 = bf16[128,1024]{1,0:T(8,128)(2,1)} copy(bf16[128,1024]{1,0:T(8,128)(2,1)} %get-tuple-element.8) | data formatting | bytes 524288
  61.4 1.7 %copy.13 = bf16[128,1024]{1,0:T(8,128)(2,1)} copy(bf16[128,1024]{1,0:T(8,128)(2,1)} %get-tuple-element.9) | data formatting | bytes 524288
  63.1 1.9 %copy.14 = bf16[1024,256]{1,0:T(8,128)(2,1)} copy(bf16[1024,256]{1,0:T(8,128)(2,1)} %get-tuple-element.10) | data formatting | bytes 1048576
  64.9 0.0 copy-done
  64.9 0.8 %copy.15 = bf16[1024,256]{1,0:T(8,128)(2,1)} copy(bf16[1024,256]{1,0:T(8,128)(2,1)S(1)} %copy-done) | data formatting | bytes 1048576
Async XLA Ops:
  59.7 5.3 %copy-start = (bf16[1024,256]{1,0:T(8,128)(2,1)S(1)}, bf16[1024,256]{1,0:T(8,128)(2,1)}, u32[]{:S(2)}) copy-start(bf16[1024,256]{1,0:T(8,128)(2,1)} %get-tuple-element.11) | copy-start | bytes 1572868
